TPU v7x, 32 devices: a whole 2x2x4 slice. The times are simulated.
32 devices in a mesh: phys: 4 (over y, x), row: 2 (over core), col: 4 (over z).
Axes of the slice: x: 2, y: 2, z: 4, core: 2. Of those that a mesh axis runs over, the one named last changes fastest.
Arguments:
- rho_sites: bfloat16 [1, 16, 2048, 2048], P(None, 'phys', 'row', 'col'), may hold values from -0.0625 to 0.0625
- sigma_sites: bfloat16 [1, 16, 2048, 2048], P(None, 'phys', 'row', 'col'), may hold values from -0.0625 to 0.0625
- environment: float32 [2048, 2048], P('row', 'col'), may hold values from -6 to 6
Outputs:
- new_environment: float32 [2048, 2048], P('row', 'col')
All inputs are finite; a program needn't handle non-finite values.
Results may differ from a plain program's by a relative error of at most 0.004.
Values may be sent and summed in bfloat16 or wider, within the bound.
A program may use at most 128 MiB of HBM per device.

v0:
```python
import functools

import jax
import jax.numpy as jnp
from jax import lax
from jax.experimental import pallas as pl
from jax.experimental.pallas import tpu as pltpu
from jax.sharding import PartitionSpec as P

MESH = pl.DeviceIdType.MESH
NCH = 4
FROM_RIGHT = {
    0: [("r", 1, k) for k in range(4)] + [("r", 2, k) for k in range(3)] + [None],
    1: [("r", 2, 0), ("r", 2, 1), ("r", 2, 2), ("r", 3, 0), ("r", 3, 1), ("r", 3, 2), ("r", 3, 3), ("r", 2, 3)],
    2: [("r", 3, k) for k in range(4)] + [("h", p) for p in range(4)],
    3: [None] * 8,
}


def mirror(item):
    if item is None or item[0] == "h":
        return item
    return ("r", 3 - item[1], item[2])


FROM_LEFT = {3 - c: [mirror(i) for i in seq] for c, seq in FROM_RIGHT.items()}
PASS_LEFT = {
    (2, 1): [(3, 0)], (2, 2): [(3, 1)], (2, 3): [(3, 2)], (2, 4): [(3, 3), (2, 3)],
    (1, 1): [(2, 0)], (1, 2): [(2, 1)], (1, 3): [(2, 2)],
}
PASS_RIGHT = {(3 - c, t): [(3 - b, k) for b, k in v] for (c, t), v in PASS_LEFT.items()}
FIRST_LEFT = {1: [(1, k) for k in range(4)], 2: [(2, 0), (2, 1), (2, 2)], 3: [(3, k) for k in range(4)]}
FIRST_RIGHT = {3 - c: [(3 - b, k) for b, k in v] for c, v in FIRST_LEFT.items()}
FOR_END = [(3, 0), (3, 1), (3, 2), (3, 3), (2, 3)]
NREM = len(FOR_END)
F32 = jnp.float32
BF16 = jnp.bfloat16


def kernel(rho_ref, sig_ref, env_ref, out_ref,
           rho_g, sig, env_f, env_g, half, half_r, acc, psend, rbuf, s1, xbuf, s2, ybuf, fin,
           rl_send, rr_send, r_recv, h_send, h_recv, loc, sg_send, sg_recv,
           el_send, er_send, e_recv, ex_send, ex_recv, ey_send, ey_recv,
           row_send, row_recv, x_send, x_recv, y_send, y_recv, o_sem, z_send, z_recv):
    ph = lax.axis_index("phys")
    r = lax.axis_index("row")
    c = lax.axis_index("col")
    width = rho_g.shape[-1]
    rows = rho_g.shape[3]
    quarter = rows // 4
    ind3 = c // 3
    ind2 = c // 2 - ind3
    ind0 = (3 - c) // 3
    ind1 = 1 - ind0 - ind2 - ind3
    inds = (ind0, ind1, ind2, ind3)

    def pick(values):
        total = 0
        for i, v in zip(inds, values):
            total = total + i * v
        return total

    mate = {"row": 1 - r}
    xn = {"phys": ph + 1 - 2 * (ph % 2)}
    yn = {"phys": (ph + 2) % 4}
    left = {"col": c - 1}
    right = {"col": c + 1}

    def remote(src, dst, ss, rs, dev):
        return pltpu.make_async_remote_copy(src_ref=src, dst_ref=dst, send_sem=ss, recv_sem=rs,
                                            device_id=dev, device_id_type=MESH)

    load_env = pltpu.make_async_copy(env_ref, env_f, loc.at[0])
    load_env.start()
    load_rho = [pltpu.make_async_copy(rho_ref.at[0, :, :, pl.ds(k * width, width)], rho_g.at[c, k], loc.at[1 + k]) for k in range(NCH)]
    for cp in load_rho:
        cp.start()
    my_rows = pl.ds(pl.multiple_of(r * rows, rows), rows)
    load_sig = pltpu.make_async_copy(sig_ref.at[0], sig.at[:, my_rows, :], loc.at[1 + NCH])
    load_sig.start()

    barrier = pltpu.get_barrier_semaphore()
    for dev in (mate, xn, yn):
        pl.semaphore_signal(barrier, inc=1, device_id=dev, device_id_type=MESH)

    @pl.when(c > 0)
    def _():
        pl.semaphore_signal(barrier, inc=1, device_id=left, device_id_type=MESH)

    @pl.when(c < 3)
    def _():
        pl.semaphore_signal(barrier, inc=1, device_id=right, device_id_type=MESH)

    load_env.wait()
    env_g[c] = env_f[...].astype(BF16)
    pl.semaphore_wait(barrier, 3 + pick((1, 2, 2, 1)))

    q_rows = pl.ds(pl.multiple_of(ph * quarter, quarter), quarter)
    h_rows = pl.ds(pl.multiple_of((ph // 2) * 2 * quarter, 2 * quarter), 2 * quarter)

    def env_left(b):
        return remote(env_g.at[b, q_rows], env_g.at[b, q_rows], el_send.at[b], e_recv.at[b], left)

    def env_right(b):
        return remote(env_g.at[b, q_rows], env_g.at[b, q_rows], er_send.at[b], e_recv.at[b], right)

    def env_x(b):
        return remote(env_g.at[b, q_rows], env_g.at[b, q_rows], ex_send.at[b], ex_recv.at[b], xn)

    def env_y(b):
        return remote(env_g.at[b, h_rows], env_g.at[b, h_rows], ey_send.at[b], ey_recv.at[b], yn)

    def send_left(b, k):
        src = rho_g.at[b, k]
        return remote(src, rho_g.at[b, k], rl_send.at[b, k], r_recv.at[b, k], left)

    def send_right(b, k):
        src = rho_g.at[b, k]
        return remote(src, rho_g.at[b, k], rr_send.at[b, k], r_recv.at[b, k], right)

    @pl.when(c > 0)
    def _():
        env_left(c).start()

    @pl.when(c < 3)
    def _():
        env_right(c).start()

    give_sig = remote(sig_ref.at[0], sig.at[:, my_rows, :], sg_send, sg_recv, mate)
    give_sig.start()
    for cp in load_rho:
        cp.wait()

    def first_sends(cols_, first, last):
        for i in cols_:
            @pl.when(c == i)
            def _():
                for b, k in FIRST_LEFT.get(i, [])[first:last]:
                    send_left(b, k).start()
                for b, k in FIRST_RIGHT.get(i, [])[first:last]:
                    send_right(b, k).start()

    first_sends((0, 3), 0, 4)
    for d in range(1, 4):
        @pl.when(c >= d)
        def _(b=c - d):
            env_right(b).wait_recv()

            @pl.when(c < 3)
            def _():
                env_right(b).start()
            env_x(b).start()

        @pl.when(c + d <= 3)
        def _(b=c + d):
            env_left(b).wait_recv()

            @pl.when(c > 0)
            def _():
                env_left(b).start()
            env_x(b).start()
        if d == 2:
            first_sends((1, 2), 0, 4)

    def others(f):
        for d in range(1, 4):
            @pl.when(c >= d)
            def _(b=c - d):
                f(b)

            @pl.when(c + d <= 3)
            def _(b=c + d):
                f(b)

    def env_y_of(b):
        env_x(b).wait_recv()
        env_y(b).start()
    others(env_y_of)
    others(lambda b: env_y(b).wait_recv())
    load_sig.wait()
    give_sig.wait_recv()

    tile = min(256, rows)

    @pl.loop(0, 4)
    def _(p):
        @pl.loop(0, rows // tile)
        def _(m):
            here = pl.ds(pl.multiple_of(m * tile, tile), tile)
            total = jnp.dot(env_g[0, here, :], sig[p, pl.ds(0, 512), :], preferred_element_type=F32)
            for b in range(1, 4):
                total += jnp.dot(env_g[b, here, :], sig[p, pl.ds(b * 512, 512), :], preferred_element_type=F32)
            half[p, here, :] = total.astype(BF16)

    def unit_of(b, k):
        return (b % 2) * NCH + k

    def product(b, k, other, unit, first=0, last=4):
        if first == 0:
            acc[unit] = jnp.zeros_like(acc.at[unit])

        @pl.loop(first, last)
        def _(p):
            acc[unit] += lax.dot_general(rho_g[b, k, p], other[p], (((0,), (0,)), ((), ())),
                                         preferred_element_type=F32)

    def row_copy(unit):
        return remote(psend.at[unit], rbuf.at[unit], row_send.at[unit], row_recv.at[unit], mate)

    def x_copy(unit):
        return remote(s1.at[unit], xbuf.at[unit], x_send.at[unit], x_recv.at[unit], xn)

    def y_copy(unit):
        return remote(s2.at[unit], ybuf.at[unit], y_send.at[unit], y_recv.at[unit], yn)

    def out_copy(unit):
        at = pl.ds(pl.multiple_of(unit * width, width), width)
        return pltpu.make_async_copy(fin.at[unit], out_ref.at[at], o_sem.at[unit])

    mid = jnp.logical_and(c > 0, c < 3)

    def end_chunk(q):
        b, k = FOR_END[q]
        return pick((0, b, 3 - b, 0)), k

    def res_left(q):
        b, k = FOR_END[q]
        return remote(fin.at[2 * NCH + q], fin.at[(b % 2) * NCH + k], z_send.at[q], z_recv.at[q], left)

    def res_right(q):
        b, k = FOR_END[q]
        return remote(fin.at[2 * NCH + q], fin.at[((3 - b) % 2) * NCH + k], z_send.at[q], z_recv.at[q], right)

    def unit_at(pos):
        _, b, k, q = pos
        return unit_of(b, k) if q is None else 2 * NCH + q

    def slot_at(pos):
        _, b, k, q = pos
        if q is not None:
            return 2 * NCH + q
        owner = b // 2
        own = 1 - (owner + r - 2 * owner * r)
        return own * unit_of(b, k) + (1 - own) * (2 * NCH + NREM)

    def stage0(pos, first=0):
        valid, b, k, q = pos

        @pl.when(valid)
        def _():
            unit, slot = unit_at(pos), slot_at(pos)
            product(b, k, half if q is None else half_r, slot, first)

            @pl.when(b // 2 != r)
            def _():
                psend[unit] = acc[slot].astype(BF16)
                row_copy(unit).start()

    def owned(pos, f):
        valid, b, k, q = pos

        @pl.when(jnp.logical_and(valid, b // 2 == r))
        def _():
            f(unit_at(pos))

    def stage1(pos):
        def f(unit):
            row_copy(unit).wait_recv()
            s1[unit] = (acc[unit] + rbuf[unit].astype(F32)).astype(BF16)
            x_copy(unit).start()
        owned(pos, f)

    def stage2(pos):
        def f(unit):
            x_copy(unit).wait_recv()
            s2[unit] = (s1[unit].astype(F32) + xbuf[unit].astype(F32)).astype(BF16)
            y_copy(unit).start()
        owned(pos, f)

    def stage3(pos):
        def f(unit):
            y_copy(unit).wait_recv()
            fin[unit] = s2[unit].astype(F32) + ybuf[unit].astype(F32)
            if pos[3] is not None:
                @pl.when(c == 1)
                def _():
                    res_left(pos[3]).start()

                @pl.when(c == 2)
                def _():
                    res_right(pos[3]).start()
            else:
                out_copy(unit).start()
        owned(pos, f)

    line = []

    def advance(pos, first=0):
        if pos is not None:
            stage0(pos, first)
        line.append(pos)
        n = len(line) - 1
        for lag, stage in ((2, stage1), (4, stage2), (6, stage3)):
            if n - lag >= 0 and line[n - lag] is not None:
                stage(line[n - lag])

    def half_copy(p, dev):
        return remote(half.at[p], half_r.at[p], h_send.at[p], h_recv.at[p], dev)

    true = c >= 0

    def arrive(t, kinds="rh"):
        for i in range(4):
            @pl.when(c == i)
            def _():
                for table, passed, send in ((FROM_RIGHT, PASS_LEFT, send_left), (FROM_LEFT, PASS_RIGHT, send_right)):
                    item = table[i][t - 1]
                    if item is None or item[0] not in kinds:
                        continue
                    if item[0] == "h":
                        half_copy(item[1], left if i == 2 else right).wait_recv()
                    else:
                        send(item[1], item[2]).wait_recv()
                    for b, k in passed.get((i, t), []):
                        send(b, k).start()

    def positions(t):
        for table in (FROM_RIGHT, FROM_LEFT):
            items = [table[i][t - 1] for i in range(4)]
            ok = [1 if it is not None and it[0] == "r" else 0 for it in items]
            blocks = [it[1] if o else 0 for it, o in zip(items, ok)]
            chunks = [it[2] if o else 0 for it, o in zip(items, ok)]
            yield (pick(ok) == 1, pick(blocks), pick(chunks), None)

    def for_end(q):
        return (mid,) + end_chunk(q) + (q,)

    def part_for_end(q, first, last):
        @pl.when(mid)
        def _():
            product(*end_chunk(q), half_r, 2 * NCH + q, first, last)

    early = {5: [(0, 0, 1), (1, 0, 1)], 6: [(0, 1, 2), (1, 1, 2), (2, 0, 2)],
             7: [(0, 2, 3), (1, 2, 3), (2, 2, 3), (3, 0, 3)]}
    arrive(1)
    for k in range(NCH):
        advance((true, c, k, None))

    @pl.when(c == 0)
    def _():
        for p in range(4):
            half_copy(p, right).start()

    @pl.when(c == 3)
    def _():
        for p in range(4):
            half_copy(p, left).start()

    for t in range(1, 8):
        if t > 1:
            arrive(t)
        for pos in positions(t):
            advance(pos)
        for q, first, last in early.get(t, []):
            part_for_end(q, first, last)
    arrive(8, "h")
    for q in range(4):
        advance(for_end(q), 3)
    arrive(8, "r")
    advance(for_end(4))
    for pos in positions(8):
        advance(pos)
    for _ in range(6):
        advance(None)

    for i, keeper, got in ((0, 1, res_left), (3, 0, res_right)):
        @pl.when(jnp.logical_and(c == i, r == keeper))
        def _():
            for q in range(NREM):
                b, k = FOR_END[q]
                got(q).wait_recv()
                out_copy(unit_of(b if i == 0 else 3 - b, k)).start()

    for unit in range(2 * NCH):
        out_copy(unit).wait()
    give_sig.wait_send()

    @pl.when(c > 0)
    def _():
        env_left(c).wait_send()

    @pl.when(c < 3)
    def _():
        env_right(c).wait_send()
    for d in range(1, 4):
        @pl.when(c >= d)
        def _(b=c - d):
            @pl.when(c < 3)
            def _():
                env_right(b).wait_send()
            env_x(b).wait_send()
            env_y(b).wait_send()

        @pl.when(c + d <= 3)
        def _(b=c + d):
            @pl.when(c > 0)
            def _():
                env_left(b).wait_send()
            env_x(b).wait_send()
            env_y(b).wait_send()
    for i in range(4):
        @pl.when(c == i)
        def _():
            for first, passed, send in ((FIRST_LEFT, PASS_LEFT, send_left), (FIRST_RIGHT, PASS_RIGHT, send_right)):
                todo = list(first.get(i, []))
                for (j, t), v in passed.items():
                    if j == i:
                        todo += v
                for b, k in todo:
                    send(b, k).wait_send()
            if i in (0, 3):
                for p in range(4):
                    half_copy(p, right if i == 0 else left).wait_send()
    for pos in line:
        if pos is None:
            continue
        valid, b, k, q = pos

        @pl.when(valid)
        def _():
            unit = unit_at(pos)

            @pl.when(b // 2 != r)
            def _():
                row_copy(unit).wait_send()

            @pl.when(b // 2 == r)
            def _():
                x_copy(unit).wait_send()
                y_copy(unit).wait_send()
                if q is not None:
                    @pl.when(c == 1)
                    def _():
                        res_left(q).wait_send()

                    @pl.when(c == 2)
                    def _():
                        res_right(q).wait_send()


def fused(rho_sites, sigma_sites, environment):
    _, pairs, rows, cols = rho_sites.shape
    width = cols // NCH
    units = 2 * NCH + NREM
    sem = pltpu.SemaphoreType.DMA
    piece = (units, width, cols)
    return pl.pallas_call(
        kernel,
        out_shape=jax.ShapeDtypeStruct(environment.shape, F32),
        in_specs=[pl.BlockSpec(memory_space=pl.ANY)] * 3,
        out_specs=pl.BlockSpec(memory_space=pl.ANY),
        scratch_shapes=[
            pltpu.VMEM((4, NCH, pairs, rows, width), BF16),
            pltpu.VMEM((pairs, 2 * rows, cols), BF16),
            pltpu.VMEM((rows, cols), F32),
            pltpu.VMEM((4, rows, cols), BF16),
            pltpu.VMEM((pairs, rows, cols), BF16),
            pltpu.VMEM((pairs, rows, cols), BF16),
            pltpu.VMEM((units + 1, width, cols), F32),
            pltpu.VMEM(piece, BF16), pltpu.VMEM(piece, BF16), pltpu.VMEM(piece, BF16),
            pltpu.VMEM(piece, BF16), pltpu.VMEM(piece, BF16), pltpu.VMEM(piece, BF16),
            pltpu.VMEM(piece, F32),
            sem((4, NCH)), sem((4, NCH)), sem((4, NCH)), sem((4,)), sem((4,)),
            sem((2 + NCH,)), sem, sem,
            sem((4,)), sem((4,)), sem((4,)), sem((4,)), sem((4,)), sem((4,)), sem((4,)),
            sem((units,)), sem((units,)), sem((units,)), sem((units,)), sem((units,)), sem((units,)),
            sem((units,)), sem((NREM,)), sem((NREM,)),
        ],
        compiler_params=pltpu.CompilerParams(
            collective_id=0, has_side_effects=True, vmem_limit_bytes=64 * 1024 * 1024 - 65536
        ),
    )(rho_sites, sigma_sites, environment)


def plain(rho_sites, sigma_sites, environment):
    env_whole = lax.all_gather(environment.astype(BF16), "col", axis=1, tiled=True)
    half = jnp.einsum(
        "ik,pkl->pil",
        env_whole,
        lax.all_gather(sigma_sites[0], "row", axis=1, tiled=True),
        preferred_element_type=F32,
    ).astype(BF16)
    partial_env = jnp.einsum(
        "pij,pil->jl",
        lax.all_gather(rho_sites[0], "col", axis=2, tiled=True),
        half,
        preferred_element_type=F32,
    )
    row_part = lax.psum_scatter(partial_env, "row", scatter_dimension=0, tiled=True)
    return lax.psum(row_part, "phys")


def solution(mesh):
    placed = (P(None, "phys", "row", "col"), P(None, "phys", "row", "col"), P("row", "col"))
    sizes = (mesh.shape["phys"], mesh.shape["row"], mesh.shape["col"])
    body = fused if sizes == (4, 2, 4) else plain
    return jax.shard_map(body, mesh=mesh, in_specs=placed, out_specs=P("row", "col"), check_vma=False)
```

profile of v0, /device:TPU:1, one launch (start us, length us, event | category | flops | bytes accessed | tf_op | source)
XLA Modules:
  0.0 222.9 jit_solution(1250394317887126769)
XLA Ops:
  0.0 219.8 %shard_map.37 = f32[1024,512]{1,0:T(8,128)} custom-call(bf16[1,4,1024,512]{3,2,1,0:T(8,128)(2,1)} %rho_ref.1, bf16[1,4,1024,512]{3,2,1,0:T(8,128)(2,1)} %sig_ref.1, f32[1024,512]{1,0:T(8,128)} %env_ref.1), custom_call_target="tpu_custom_call" | custom-call | tf_op jit(solution)/shard_map/pallas_call | solution.py:457
  219.8 3.1 %copy.5 = f32[1024,512]{1,0:T(8,128)} copy(f32[1024,512]{1,0:T(8,128)} %shard_map.37) | data formatting | bytes 4194304
where the time goes:
time: 224 us; the launch traced here: 223 us
  Pallas kernels  220 us (98%)
  local copies, waits for them, and re-layouts  3.08 us (1%)
    pallas_call x1, Pallas kernels, fused(): pl.pallas_call(kernel, out_shape=jax.ShapeDtypeStruct(environment.shape,...  220 us

commit v1 on v0

--- a/solution.py
+++ b/solution.py
@@ -38,10 +38,10 @@
 
 
 def kernel(rho_ref, sig_ref, env_ref, out_ref,
-           rho_g, sig, env_f, env_g, half, half_r, acc, psend, rbuf, s1, xbuf, s2, ybuf, fin,
-           rl_send, rr_send, r_recv, h_send, h_recv, loc, sg_send, sg_recv,
+           rho_g, sig, env_f, env_g, half, half_r, acc, psend, rbuf, s1, f1, s2, f2,
+           rl_send, rr_send, r_recv, l_send, l_recv, h_send, h_recv, loc, sg_send, sg_recv,
            el_send, er_send, e_recv, ex_send, ex_recv, ey_send, ey_recv,
-           row_send, row_recv, x_send, x_recv, y_send, y_recv, o_sem, z_send, z_recv):
+           row_send, row_recv, x_send, x_recv, y_send, y_recv, z_send, z_recv):
     ph = lax.axis_index("phys")
     r = lax.axis_index("row")
     c = lax.axis_index("col")
@@ -65,6 +65,9 @@
     yn = {"phys": (ph + 2) % 4}
     left = {"col": c - 1}
     right = {"col": c + 1}
+    mid = jnp.logical_and(c > 0, c < 3)
+    middle = {"col": 3 - c}
+    end = {"col": 3 * (c // 2)}
 
     def remote(src, dst, ss, rs, dev):
         return pltpu.make_async_remote_copy(src_ref=src, dst_ref=dst, send_sem=ss, recv_sem=rs,
@@ -111,12 +114,18 @@
         return remote(env_g.at[b, h_rows], env_g.at[b, h_rows], ey_send.at[b], ey_recv.at[b], yn)
 
     def send_left(b, k):
-        src = rho_g.at[b, k]
-        return remote(src, rho_g.at[b, k], rl_send.at[b, k], r_recv.at[b, k], left)
+        return remote(rho_g.at[b, k], rho_g.at[b, k], rl_send.at[b, k], r_recv.at[b, k], left)
 
     def send_right(b, k):
-        src = rho_g.at[b, k]
-        return remote(src, rho_g.at[b, k], rr_send.at[b, k], r_recv.at[b, k], right)
+        return remote(rho_g.at[b, k], rho_g.at[b, k], rr_send.at[b, k], r_recv.at[b, k], right)
+
+    def first_piece(p):
+        at = rho_g.at[c, 0, p]
+        remote(at, at, rl_send.at[c, 0], r_recv.at[c, 0], left).start()
+        remote(at, at, rr_send.at[c, 0], r_recv.at[c, 0], right).start()
+
+    def last_piece(b, p):
+        return remote(rho_g.at[b, NCH - 1, p], rho_g.at[b, NCH - 1, p], l_send.at[p], l_recv.at[p], middle)
 
     @pl.when(c > 0)
     def _():
@@ -127,20 +136,29 @@
         env_right(c).start()
 
     give_sig = remote(sig_ref.at[0], sig.at[:, my_rows, :], sg_send, sg_recv, mate)
+    load_rho[0].wait()
+
+    @pl.when(mid)
+    def _():
+        first_piece(0)
     give_sig.start()
-    for cp in load_rho:
-        cp.wait()
-
-    def first_sends(cols_, first, last):
-        for i in cols_:
+
+    def first_sends(i, k):
+        for b, kk in FIRST_LEFT.get(i, []):
+            if kk == k:
+                send_left(b, k).start()
+        for b, kk in FIRST_RIGHT.get(i, []):
+            if kk == k:
+                send_right(b, k).start()
+
+    for k in range(NCH):
+        if k:
+            load_rho[k].wait()
+        for i in (0, 3):
             @pl.when(c == i)
             def _():
-                for b, k in FIRST_LEFT.get(i, [])[first:last]:
-                    send_left(b, k).start()
-                for b, k in FIRST_RIGHT.get(i, [])[first:last]:
-                    send_right(b, k).start()
-
-    first_sends((0, 3), 0, 4)
+                first_sends(i, k)
+
     for d in range(1, 4):
         @pl.when(c >= d)
         def _(b=c - d):
@@ -159,8 +177,20 @@
             def _():
                 env_left(b).start()
             env_x(b).start()
+        if d == 1:
+            @pl.when(mid)
+            def _():
+                first_piece(1)
         if d == 2:
-            first_sends((1, 2), 0, 4)
+            @pl.when(mid)
+            def _():
+                first_piece(2)
+                first_piece(3)
+            for i in (1, 2):
+                @pl.when(c == i)
+                def _():
+                    for k in range(1, NCH):
+                        first_sends(i, k)
 
     def others(f):
         for d in range(1, 4):
@@ -204,32 +234,35 @@
             acc[unit] += lax.dot_general(rho_g[b, k, p], other[p], (((0,), (0,)), ((), ())),
                                          preferred_element_type=F32)
 
+    part_a = pl.ds(0, width // 2)
+    part_b = pl.ds(width // 2, width // 2)
+
     def row_copy(unit):
         return remote(psend.at[unit], rbuf.at[unit], row_send.at[unit], row_recv.at[unit], mate)
 
-    def x_copy(unit):
-        return remote(s1.at[unit], xbuf.at[unit], x_send.at[unit], x_recv.at[unit], xn)
-
-    def y_copy(unit):
-        return remote(s2.at[unit], ybuf.at[unit], y_send.at[unit], y_recv.at[unit], yn)
-
-    def out_copy(unit):
-        at = pl.ds(pl.multiple_of(unit * width, width), width)
-        return pltpu.make_async_copy(fin.at[unit], out_ref.at[at], o_sem.at[unit])
-
-    mid = jnp.logical_and(c > 0, c < 3)
+    def one_x(u):
+        return remote(s1.at[u, part_a], f1.at[u, part_a], x_send.at[u, 0], x_recv.at[u, 0], xn)
+
+    def one_y(u):
+        return remote(s1.at[u, part_b], f1.at[u, part_b], y_send.at[u, 0], y_recv.at[u, 0], yn)
+
+    def two_y(u):
+        return remote(s2.at[u, part_a], f2.at[u, part_a], y_send.at[u, 1], y_recv.at[u, 1], yn)
+
+    def two_x(u):
+        return remote(s2.at[u, part_b], f2.at[u, part_b], x_send.at[u, 1], x_recv.at[u, 1], xn)
 
     def end_chunk(q):
         b, k = FOR_END[q]
         return pick((0, b, 3 - b, 0)), k
 
-    def res_left(q):
+    def end_unit(q):
         b, k = FOR_END[q]
-        return remote(fin.at[2 * NCH + q], fin.at[(b % 2) * NCH + k], z_send.at[q], z_recv.at[q], left)
-
-    def res_right(q):
-        b, k = FOR_END[q]
-        return remote(fin.at[2 * NCH + q], fin.at[((3 - b) % 2) * NCH + k], z_send.at[q], z_recv.at[q], right)
+        there, mirrored = unit_of(b, k), unit_of(3 - b, k)
+        return pick((there, there, mirrored, mirrored))
+
+    def z_copy(q):
+        return remote(s1.at[2 * NCH + q], s1.at[end_unit(q)], z_send.at[q], z_recv.at[q], end)
 
     def unit_at(pos):
         _, b, k, q = pos
@@ -243,18 +276,19 @@
         own = 1 - (owner + r - 2 * owner * r)
         return own * unit_of(b, k) + (1 - own) * (2 * NCH + NREM)
 
+    def to_mate(pos):
+        @pl.when(pos[1] // 2 != r)
+        def _():
+            psend[unit_at(pos)] = acc[slot_at(pos)].astype(BF16)
+            row_copy(unit_at(pos)).start()
+
     def stage0(pos, first=0):
         valid, b, k, q = pos
 
         @pl.when(valid)
         def _():
-            unit, slot = unit_at(pos), slot_at(pos)
-            product(b, k, half if q is None else half_r, slot, first)
-
-            @pl.when(b // 2 != r)
-            def _():
-                psend[unit] = acc[slot].astype(BF16)
-                row_copy(unit).start()
+            product(b, k, half if q is None else half_r, slot_at(pos), first)
+            to_mate(pos)
 
     def owned(pos, f):
         valid, b, k, q = pos
@@ -262,67 +296,72 @@
         @pl.when(jnp.logical_and(valid, b // 2 == r))
         def _():
             f(unit_at(pos))
+
+    def begin(u):
+        one_x(u).start()
+        one_y(u).start()
+
+    def turn(u):
+        one_x(u).wait_recv()
+        s2[u, part_a] = (s1[u, part_a].astype(F32) + f1[u, part_a].astype(F32)).astype(BF16)
+        two_y(u).start()
+        one_y(u).wait_recv()
+        s2[u, part_b] = (s1[u, part_b].astype(F32) + f1[u, part_b].astype(F32)).astype(BF16)
+        two_x(u).start()
+
+    def finish(u):
+        two_y(u).wait_recv()
+        two_x(u).wait_recv()
+        at = pl.ds(pl.multiple_of(u * width, width), width)
+        out_ref[at, :] = s2[u].astype(F32) + f2[u].astype(F32)
 
     def stage1(pos):
         def f(unit):
             row_copy(unit).wait_recv()
             s1[unit] = (acc[unit] + rbuf[unit].astype(F32)).astype(BF16)
-            x_copy(unit).start()
+            if pos[3] is None:
+                begin(unit)
+            else:
+                z_copy(pos[3]).start()
         owned(pos, f)
 
-    def stage2(pos):
-        def f(unit):
-            x_copy(unit).wait_recv()
-            s2[unit] = (s1[unit].astype(F32) + xbuf[unit].astype(F32)).astype(BF16)
-            y_copy(unit).start()
-        owned(pos, f)
-
-    def stage3(pos):
-        def f(unit):
-            y_copy(unit).wait_recv()
-            fin[unit] = s2[unit].astype(F32) + ybuf[unit].astype(F32)
-            if pos[3] is not None:
-                @pl.when(c == 1)
-                def _():
-                    res_left(pos[3]).start()
-
-                @pl.when(c == 2)
-                def _():
-                    res_right(pos[3]).start()
-            else:
-                out_copy(unit).start()
-        owned(pos, f)
-
     line = []
 
-    def advance(pos, first=0):
+    def advance(pos):
         if pos is not None:
-            stage0(pos, first)
+            stage0(pos)
         line.append(pos)
         n = len(line) - 1
-        for lag, stage in ((2, stage1), (4, stage2), (6, stage3)):
-            if n - lag >= 0 and line[n - lag] is not None:
-                stage(line[n - lag])
+        if n >= 2 and line[n - 2] is not None:
+            stage1(line[n - 2])
+        if n >= 4 and line[n - 4] is not None:
+            owned(line[n - 4], turn)
+        if n >= 6 and line[n - 6] is not None:
+            owned(line[n - 6], finish)
 
     def half_copy(p, dev):
         return remote(half.at[p], half_r.at[p], h_send.at[p], h_recv.at[p], dev)
 
     true = c >= 0
 
-    def arrive(t, kinds="rh"):
+    def arrive(t):
         for i in range(4):
             @pl.when(c == i)
             def _():
                 for table, passed, send in ((FROM_RIGHT, PASS_LEFT, send_left), (FROM_LEFT, PASS_RIGHT, send_right)):
                     item = table[i][t - 1]
-                    if item is None or item[0] not in kinds:
+                    if item is None:
                         continue
                     if item[0] == "h":
                         half_copy(item[1], left if i == 2 else right).wait_recv()
                     else:
                         send(item[1], item[2]).wait_recv()
                     for b, k in passed.get((i, t), []):
-                        send(b, k).start()
+                        if b == i:
+                            for p in range(4):
+                                last_piece(c, p).start()
+                        else:
+                            send(b, k).start()
 
     def positions(t):
         for table in (FROM_RIGHT, FROM_LEFT):
@@ -363,26 +402,51 @@
             advance(pos)
         for q, first, last in early.get(t, []):
             part_for_end(q, first, last)
-    arrive(8, "h")
-    for q in range(4):
-        advance(for_end(q), 3)
-    arrive(8, "r")
-    advance(for_end(4))
-    for pos in positions(8):
-        advance(pos)
     for _ in range(6):
         advance(None)
 
-    for i, keeper, got in ((0, 1, res_left), (3, 0, res_right)):
-        @pl.when(jnp.logical_and(c == i, r == keeper))
-        def _():
-            for q in range(NREM):
-                b, k = FOR_END[q]
-                got(q).wait_recv()
-                out_copy(unit_of(b if i == 0 else 3 - b, k)).start()
-
-    for unit in range(2 * NCH):
-        out_copy(unit).wait()
+    own_last = (mid, 3 - c, NCH - 1, None)
+    end_last = for_end(NREM - 1)
+
+    def last_products(p):
+        last_piece(3 - c, p).wait_recv()
+        product(3 - c, NCH - 1, half_r, slot_at(end_last), p, p + 1)
+        if p == 3:
+            to_mate(end_last)
+        product(3 - c, NCH - 1, half, slot_at(own_last), p, p + 1)
+        if p == 3:
+            to_mate(own_last)
+
+    @pl.when(mid)
+    def _():
+        last_products(0)
+        last_products(1)
+        half_copy(3, middle).wait_recv()
+        for q in range(NREM - 1):
+            stage0(for_end(q), 3)
+        for q in range(NREM - 1):
+            stage1(for_end(q))
+        last_products(2)
+        last_products(3)
+        stage1(end_last)
+        stage1(own_last)
+        owned(own_last, turn)
+        owned(own_last, finish)
+
+    keeper = jnp.logical_or(jnp.logical_and(c == 0, r == 1), jnp.logical_and(c == 3, r == 0))
+
+    @pl.when(keeper)
+    def _():
+        for step, q in (("z", 0), ("z", 1), ("t", 0), ("z", 2), ("t", 1), ("f", 0), ("z", 3), ("t", 2), ("f", 1),
+                        ("t", 3), ("z", 4), ("f", 2), ("f", 3), ("t", 4), ("f", 4)):
+            if step == "z":
+                z_copy(q).wait_recv()
+                begin(end_unit(q))
+            elif step == "t":
+                turn(end_unit(q))
+            else:
+                finish(end_unit(q))
+
     give_sig.wait_send()
 
     @pl.when(c > 0)
@@ -415,50 +479,56 @@
                 todo = list(first.get(i, []))
                 for (j, t), v in passed.items():
                     if j == i:
-                        todo += v
+                        todo += [(b, k) for b, k in v if b != i]
                 for b, k in todo:
                     send(b, k).wait_send()
             if i in (0, 3):
                 for p in range(4):
                     half_copy(p, right if i == 0 else left).wait_send()
-    for pos in line:
-        if pos is None:
-            continue
-        valid, b, k, q = pos
-
-        @pl.when(valid)
+            else:
+                for p in range(4):
+                    last_piece(c, p).wait_send()
+
+    def exchanged(u):
+        one_x(u).wait_send()
+        one_y(u).wait_send()
+        two_y(u).wait_send()
+        two_x(u).wait_send()
+
+    for pos in [pos for pos in line if pos is not None] + [own_last] + [for_end(q) for q in range(NREM)]:
+        @pl.when(pos[0])
         def _():
             unit = unit_at(pos)
 
-            @pl.when(b // 2 != r)
+            @pl.when(pos[1] // 2 != r)
             def _():
                 row_copy(unit).wait_send()
 
-            @pl.when(b // 2 == r)
-            def _():
-                x_copy(unit).wait_send()
-                y_copy(unit).wait_send()
-                if q is not None:
-                    @pl.when(c == 1)
-                    def _():
-                        res_left(q).wait_send()
-
-                    @pl.when(c == 2)
-                    def _():
-                        res_right(q).wait_send()
+            @pl.when(pos[1] // 2 == r)
+            def _():
+                if pos[3] is None:
+                    exchanged(unit)
+                else:
+                    z_copy(pos[3]).wait_send()
+
+    @pl.when(keeper)
+    def _():
+        for q in range(NREM):
+            exchanged(end_unit(q))
 
 
 def fused(rho_sites, sigma_sites, environment):
     _, pairs, rows, cols = rho_sites.shape
     width = cols // NCH
-    units = 2 * NCH + NREM
+    units = 2 * NCH
     sem = pltpu.SemaphoreType.DMA
-    piece = (units, width, cols)
+    piece = (units + NREM, width, cols)
+    pair = (units, width, cols)
     return pl.pallas_call(
         kernel,
-        out_shape=jax.ShapeDtypeStruct(environment.shape, F32),
+        out_shape=pltpu.VMEM(environment.shape, F32),
         in_specs=[pl.BlockSpec(memory_space=pl.ANY)] * 3,
-        out_specs=pl.BlockSpec(memory_space=pl.ANY),
+        out_specs=pl.BlockSpec(memory_space=pltpu.VMEM),
         scratch_shapes=[
             pltpu.VMEM((4, NCH, pairs, rows, width), BF16),
             pltpu.VMEM((pairs, 2 * rows, cols), BF16),
@@ -466,18 +536,18 @@
             pltpu.VMEM((4, rows, cols), BF16),
             pltpu.VMEM((pairs, rows, cols), BF16),
             pltpu.VMEM((pairs, rows, cols), BF16),
-            pltpu.VMEM((units + 1, width, cols), F32),
+            pltpu.VMEM((units + NREM + 1, width, cols), F32),
             pltpu.VMEM(piece, BF16), pltpu.VMEM(piece, BF16), pltpu.VMEM(piece, BF16),
-            pltpu.VMEM(piece, BF16), pltpu.VMEM(piece, BF16), pltpu.VMEM(piece, BF16),
-            pltpu.VMEM(piece, F32),
-            sem((4, NCH)), sem((4, NCH)), sem((4, NCH)), sem((4,)), sem((4,)),
+            pltpu.VMEM(pair, BF16), pltpu.VMEM(pair, BF16), pltpu.VMEM(pair, BF16),
+            sem((4, NCH)), sem((4, NCH)), sem((4, NCH)), sem((4,)), sem((4,)), sem((4,)), sem((4,)),
             sem((2 + NCH,)), sem, sem,
             sem((4,)), sem((4,)), sem((4,)), sem((4,)), sem((4,)), sem((4,)), sem((4,)),
-            sem((units,)), sem((units,)), sem((units,)), sem((units,)), sem((units,)), sem((units,)),
-            sem((units,)), sem((NREM,)), sem((NREM,)),
+            sem((units + NREM,)), sem((units + NREM,)),
+            sem((units, 2)), sem((units, 2)), sem((units, 2)), sem((units, 2)),
+            sem((NREM,)), sem((NREM,)),
         ],
         compiler_params=pltpu.CompilerParams(
-            collective_id=0, has_side_effects=True, vmem_limit_bytes=64 * 1024 * 1024 - 65536
+            collective_id=0, has_side_effects=True, vmem_limit_bytes=58 * 1024 * 1024
         ),
     )(rho_sites, sigma_sites, environment)
 

time: 224 us -> 215 us (0.960); the launches traced: 223 us -> 212 us
  Pallas kernels: 220 us -> 210 us
    pallas_call x1, Pallas kernels: 220 us -> 210 us  [fused(): pl.pallas_call(kernel, out_shape=pltpu.VMEM(environment.shape, F32), in_s...]
where the time goes in v1:
time: 215 us; the launch traced here: 212 us
  Pallas kernels  210 us (98%)
    pallas_call x1, Pallas kernels, fused(): pl.pallas_call(kernel, out_shape=pltpu.VMEM(environment.shape, F32), in_s...  210 us

profile of v1, /device:TPU:1, one launch (start us, length us, event | category | flops | bytes accessed | tf_op | source)
XLA Modules:
  0.0 211.5 jit_solution(15690671774660893904)
XLA Ops:
  0.0 210.2 %shard_map.37 = f32[1024,512]{1,0:T(8,128)S(1)} custom-call(bf16[1,4,1024,512]{3,2,1,0:T(8,128)(2,1)} %rho_ref.1, bf16[1,4,1024,512]{3,2,1,0:T(8,128)(2,1)} %sig_ref.1, f32[1024,512]{1,0:T(8,128)} %env_ref.1), custom_call_target="tpu_custom_call" | custom-call | tf_op jit(solution)/shard_map/pallas_call | solution.py:527
  210.2 1.3 copy.5

commit v2 on v1

--- a/solution.py
+++ b/solution.py
@@ -10,10 +10,10 @@
 MESH = pl.DeviceIdType.MESH
 NCH = 4
 FROM_RIGHT = {
-    0: [("r", 1, k) for k in range(4)] + [("r", 2, k) for k in range(3)] + [None],
-    1: [("r", 2, 0), ("r", 2, 1), ("r", 2, 2), ("r", 3, 0), ("r", 3, 1), ("r", 3, 2), ("r", 3, 3), ("r", 2, 3)],
-    2: [("r", 3, k) for k in range(4)] + [("h", p) for p in range(4)],
-    3: [None] * 8,
+    0: [("r", 1, k) for k in range(4)] + [None] * 3,
+    1: [("r", 2, 0), ("r", 2, 1), ("r", 2, 2), ("r", 3, 0), ("r", 3, 1), ("r", 3, 2), ("r", 3, 3)],
+    2: [("r", 3, k) for k in range(4)] + [("h", p) for p in range(3)],
+    3: [None] * 7,
 }
 
 
@@ -24,21 +24,20 @@
 
 
 FROM_LEFT = {3 - c: [mirror(i) for i in seq] for c, seq in FROM_RIGHT.items()}
-PASS_LEFT = {
-    (2, 1): [(3, 0)], (2, 2): [(3, 1)], (2, 3): [(3, 2)], (2, 4): [(3, 3), (2, 3)],
-    (1, 1): [(2, 0)], (1, 2): [(2, 1)], (1, 3): [(2, 2)],
-}
+PASS_LEFT = {(2, 1): [(3, 0)], (2, 2): [(3, 1)], (2, 3): [(3, 2)], (2, 4): [(3, 3), (2, 3)]}
 PASS_RIGHT = {(3 - c, t): [(3 - b, k) for b, k in v] for (c, t), v in PASS_LEFT.items()}
 FIRST_LEFT = {1: [(1, k) for k in range(4)], 2: [(2, 0), (2, 1), (2, 2)], 3: [(3, k) for k in range(4)]}
 FIRST_RIGHT = {3 - c: [(3 - b, k) for b, k in v] for c, v in FIRST_LEFT.items()}
-FOR_END = [(3, 0), (3, 1), (3, 2), (3, 3), (2, 3)]
+FOR_END = [(2, 0), (2, 1), (2, 2), (3, 0), (3, 1), (3, 2), (3, 3), (2, 3)]
 NREM = len(FOR_END)
+SPLIT = 3
+LAST_ORDER = (3, 0, 1, 2)
 F32 = jnp.float32
 BF16 = jnp.bfloat16
 
 
 def kernel(rho_ref, sig_ref, env_ref, out_ref,
-           rho_g, sig, env_f, env_g, half, half_r, acc, psend, rbuf, s1, f1, s2, f2,
+           rho_g, sig, env_f, env_g, half, half_r, acc, psend, rbuf, s1, f1, s2, f2, zbuf,
            rl_send, rr_send, r_recv, l_send, l_recv, h_send, h_recv, loc, sg_send, sg_recv,
            el_send, er_send, e_recv, ex_send, ex_recv, ey_send, ey_recv,
            row_send, row_recv, x_send, x_recv, y_send, y_recv, z_send, z_recv):
@@ -124,6 +123,10 @@
         remote(at, at, rl_send.at[c, 0], r_recv.at[c, 0], left).start()
         remote(at, at, rr_send.at[c, 0], r_recv.at[c, 0], right).start()
 
+    def pass_piece(b, k, dev):
+        at = rho_g.at[b, k, SPLIT]
+        return remote(at, at, rl_send.at[b, k], r_recv.at[b, k], dev)
+
     def last_piece(b, p):
         return remote(rho_g.at[b, NCH - 1, p], rho_g.at[b, NCH - 1, p], l_send.at[p], l_recv.at[p], middle)
 
@@ -225,8 +228,8 @@
     def unit_of(b, k):
         return (b % 2) * NCH + k
 
-    def product(b, k, other, unit, first=0, last=4):
-        if first == 0:
+    def product(b, k, other, unit, first=0, last=4, zero=None):
+        if zero or (zero is None and first == 0):
             acc[unit] = jnp.zeros_like(acc.at[unit])
 
         @pl.loop(first, last)
@@ -254,7 +257,7 @@
 
     def end_chunk(q):
         b, k = FOR_END[q]
-        return pick((0, b, 3 - b, 0)), k
+        return pick((b, b, 3 - b, 3 - b)), k
 
     def end_unit(q):
         b, k = FOR_END[q]
@@ -262,7 +265,10 @@
         return pick((there, there, mirrored, mirrored))
 
     def z_copy(q):
-        return remote(s1.at[2 * NCH + q], s1.at[end_unit(q)], z_send.at[q], z_recv.at[q], end)
+        return remote(s1.at[2 * NCH + q], zbuf.at[end_unit(q)], z_send.at[q], z_recv.at[q], end)
+
+    def end_piece(q):
+        return pass_piece(*end_chunk(q), end)
 
     def unit_at(pos):
         _, b, k, q = pos
@@ -344,24 +350,34 @@
 
     true = c >= 0
 
-    def arrive(t):
+    def arrive(t, kinds="rh"):
         for i in range(4):
             @pl.when(c == i)
             def _():
-                for table, passed, send in ((FROM_RIGHT, PASS_LEFT, send_left), (FROM_LEFT, PASS_RIGHT, send_right)):
+                for table, passed, send, on in ((FROM_RIGHT, PASS_LEFT, send_left, 1), (FROM_LEFT, PASS_RIGHT, send_right, 2)):
                     item = table[i][t - 1]
-                    if item is None:
+                    if item is None or item[0] not in kinds:
                         continue
                     if item[0] == "h":
                         half_copy(item[1], left if i == 2 else right).wait_recv()
                     else:
                         send(item[1], item[2]).wait_recv()
-                    for b, k in passed.get((i, t), []):
-                        if b == i:
-                            for p in range(4):
-                                last_piece(c, p).start()
-                        else:
-                            send(b, k).start()
+                        if i == on:
+                            pass_piece(item[1], item[2], end).start()
+                        for b, k in passed.get((i, t), []):
+                            if b == i:
+                                for p in LAST_ORDER:
+                                    last_piece(c, p).start()
+                            else:
+                                send(b, k).start()
+
+    def for_end(q):
+        return (mid,) + end_chunk(q) + (q,)
+
+    def part_for_end(q, first, last):
+        @pl.when(mid)
+        def _():
+            product(*end_chunk(q), half_r, 2 * NCH + q, first, last)
 
     def positions(t):
         for table in (FROM_RIGHT, FROM_LEFT):
@@ -371,123 +387,57 @@
             chunks = [it[2] if o else 0 for it, o in zip(items, ok)]
             yield (pick(ok) == 1, pick(blocks), pick(chunks), None)
 
-    def for_end(q):
-        return (mid,) + end_chunk(q) + (q,)
-
-    def part_for_end(q, first, last):
-        @pl.when(mid)
-        def _():
-            product(*end_chunk(q), half_r, 2 * NCH + q, first, last)
-
-    early = {5: [(0, 0, 1), (1, 0, 1)], 6: [(0, 1, 2), (1, 1, 2), (2, 0, 2)],
-             7: [(0, 2, 3), (1, 2, 3), (2, 2, 3), (3, 0, 3)]}
     arrive(1)
     for k in range(NCH):
         advance((true, c, k, None))
 
     @pl.when(c == 0)
     def _():
-        for p in range(4):
+        for p in range(SPLIT):
             half_copy(p, right).start()
 
     @pl.when(c == 3)
     def _():
-        for p in range(4):
+        for p in range(SPLIT):
             half_copy(p, left).start()
 
-    for t in range(1, 8):
+    for t in range(1, 7):
         if t > 1:
             arrive(t)
         for pos in positions(t):
             advance(pos)
-        for q, first, last in early.get(t, []):
-            part_for_end(q, first, last)
+        if t == 5:
+            for q in range(5):
+                part_for_end(q, 0, 1)
+        if t == 6:
+            for q in range(5):
+                part_for_end(q, 1, 2)
+            part_for_end(5, 0, 2)
+    arrive(7, "h")
+
+    @pl.when(mid)
+    def _():
+        for q in range(6):
+            product(*end_chunk(q), half_r, 2 * NCH + q, 2, 3)
+            to_mate(for_end(q))
+        for q in range(6):
+            stage1(for_end(q))
+    arrive(7, "r")
+    for pos in positions(7):
+        advance(pos)
+
+    @pl.when(mid)
+    def _():
+        product(*end_chunk(6), half_r, 2 * NCH + 6, 0, 3)
+        to_mate(for_end(6))
+        stage1(for_end(6))
     for _ in range(6):
         advance(None)
 
     own_last = (mid, 3 - c, NCH - 1, None)
     end_last = for_end(NREM - 1)
-
-    def last_products(p):
-        last_piece(3 - c, p).wait_recv()
-        product(3 - c, NCH - 1, half_r, slot_at(end_last), p, p + 1)
-        if p == 3:
-            to_mate(end_last)
-        product(3 - c, NCH - 1, half, slot_at(own_last), p, p + 1)
-        if p == 3:
-            to_mate(own_last)
-
-    @pl.when(mid)
-    def _():
-        last_products(0)
-        last_products(1)
-        half_copy(3, middle).wait_recv()
-        for q in range(NREM - 1):
-            stage0(for_end(q), 3)
-        for q in range(NREM - 1):
-            stage1(for_end(q))
-        last_products(2)
-        last_products(3)
-        stage1(end_last)
-        stage1(own_last)
-        owned(own_last, turn)
-        owned(own_last, finish)
-
+    at_end = jnp.logical_or(c == 0, c == 3)
     keeper = jnp.logical_or(jnp.logical_and(c == 0, r == 1), jnp.logical_and(c == 3, r == 0))
-
-    @pl.when(keeper)
-    def _():
-        for step, q in (("z", 0), ("z", 1), ("t", 0), ("z", 2), ("t", 1), ("f", 0), ("z", 3), ("t", 2), ("f", 1),
-                        ("t", 3), ("z", 4), ("f", 2), ("f", 3), ("t", 4), ("f", 4)):
-            if step == "z":
-                z_copy(q).wait_recv()
-                begin(end_unit(q))
-            elif step == "t":
-                turn(end_unit(q))
-            else:
-                finish(end_unit(q))
-
-    give_sig.wait_send()
-
-    @pl.when(c > 0)
-    def _():
-        env_left(c).wait_send()
-
-    @pl.when(c < 3)
-    def _():
-        env_right(c).wait_send()
-    for d in range(1, 4):
-        @pl.when(c >= d)
-        def _(b=c - d):
-            @pl.when(c < 3)
-            def _():
-                env_right(b).wait_send()
-            env_x(b).wait_send()
-            env_y(b).wait_send()
-
-        @pl.when(c + d <= 3)
-        def _(b=c + d):
-            @pl.when(c > 0)
-            def _():
-                env_left(b).wait_send()
-            env_x(b).wait_send()
-            env_y(b).wait_send()
-    for i in range(4):
-        @pl.when(c == i)
-        def _():
-            for first, passed, send in ((FIRST_LEFT, PASS_LEFT, send_left), (FIRST_RIGHT, PASS_RIGHT, send_right)):
-                todo = list(first.get(i, []))
-                for (j, t), v in passed.items():
-                    if j == i:
-                        todo += [(b, k) for b, k in v if b != i]
-                for b, k in todo:
-                    send(b, k).wait_send()
-            if i in (0, 3):
-                for p in range(4):
-                    half_copy(p, right if i == 0 else left).wait_send()
-            else:
-                for p in range(4):
-                    last_piece(c, p).wait_send()
 
     def exchanged(u):
         one_x(u).wait_send()
@@ -495,7 +445,7 @@
         two_y(u).wait_send()
         two_x(u).wait_send()
 
-    for pos in [pos for pos in line if pos is not None] + [own_last] + [for_end(q) for q in range(NREM)]:
+    def sent(pos):
         @pl.when(pos[0])
         def _():
             unit = unit_at(pos)
@@ -511,10 +461,131 @@
                 else:
                     z_copy(pos[3]).wait_send()
 
-    @pl.when(keeper)
-    def _():
-        for q in range(NREM):
-            exchanged(end_unit(q))
+    def settle():
+        give_sig.wait_send()
+
+        @pl.when(c > 0)
+        def _():
+            env_left(c).wait_send()
+
+        @pl.when(c < 3)
+        def _():
+            env_right(c).wait_send()
+        for d in range(1, 4):
+            @pl.when(c >= d)
+            def _(b=c - d):
+                @pl.when(c < 3)
+                def _():
+                    env_right(b).wait_send()
+                env_x(b).wait_send()
+                env_y(b).wait_send()
+
+            @pl.when(c + d <= 3)
+            def _(b=c + d):
+                @pl.when(c > 0)
+                def _():
+                    env_left(b).wait_send()
+                env_x(b).wait_send()
+                env_y(b).wait_send()
+        for i in range(4):
+            @pl.when(c == i)
+            def _():
+                for first, passed, send in ((FIRST_LEFT, PASS_LEFT, send_left), (FIRST_RIGHT, PASS_RIGHT, send_right)):
+                    todo = list(first.get(i, []))
+                    for (j, t), v in passed.items():
+                        if j == i:
+                            todo += [(b, k) for b, k in v if b != i]
+                    for b, k in todo:
+                        send(b, k).wait_send()
+                if i in (0, 3):
+                    for p in range(SPLIT):
+                        half_copy(p, right if i == 0 else left).wait_send()
+        for pos in line:
+            if pos is not None:
+                sent(pos)
+
+    @pl.when(mid)
+    def _():
+        settle()
+
+    def last_products(p):
+        last_piece(3 - c, p).wait_recv()
+        first, final = p == LAST_ORDER[0], p == LAST_ORDER[-1]
+        if p == SPLIT:
+            end_piece(NREM - 1).start()
+        else:
+            product(3 - c, NCH - 1, half_r, slot_at(end_last), p, p + 1)
+        if final:
+            to_mate(end_last)
+        product(3 - c, NCH - 1, half, slot_at(own_last), p, p + 1, zero=first)
+        if final:
+            to_mate(own_last)
+
+    @pl.when(mid)
+    def _():
+        for q in range(6):
+            end_piece(q).wait_send()
+            sent(for_end(q))
+        for p in LAST_ORDER:
+            last_products(p)
+        stage1(end_last)
+        stage1(own_last)
+        owned(own_last, turn)
+        owned(own_last, finish)
+        end_piece(6).wait_send()
+        end_piece(7).wait_send()
+        sent(for_end(6))
+        sent(end_last)
+        sent(own_last)
+        for p in LAST_ORDER:
+            last_piece(c, p).wait_send()
+
+    def end_part(q):
+        pos = (at_end,) + end_chunk(q) + (None,)
+        end_piece(q).wait_recv()
+        product(pos[1], pos[2], half, slot_at(pos), SPLIT, SPLIT + 1, zero=True)
+        to_mate(pos)
+
+    def gather(q):
+        u = end_unit(q)
+        row_copy(u).wait_recv()
+        z_copy(q).wait_recv()
+        s1[u] = (acc[u] + rbuf[u].astype(F32) + zbuf[u].astype(F32)).astype(BF16)
+        begin(u)
+
+    @pl.when(at_end)
+    def _():
+        for q in range(NREM - 2):
+            end_part(q)
+        settle()
+
+        @pl.when(keeper)
+        def _():
+            for n in range(NREM - 2 + 4):
+                if n < NREM - 2:
+                    gather(n)
+                if 0 <= n - 2 < NREM - 2:
+                    turn(end_unit(n - 2))
+                if 0 <= n - 4:
+                    finish(end_unit(n - 4))
+            for q in range(NREM - 2):
+                exchanged(end_unit(q))
+        for q in (NREM - 2, NREM - 1):
+            end_part(q)
+
+        @pl.when(keeper)
+        def _():
+            for q in (NREM - 2, NREM - 1):
+                gather(q)
+                turn(end_unit(q))
+                finish(end_unit(q))
+            for q in (NREM - 2, NREM - 1):
+                exchanged(end_unit(q))
+
+        @pl.when(jnp.logical_not(keeper))
+        def _():
+            for q in range(NREM):
+                row_copy(end_unit(q)).wait_send()
 
 
 def fused(rho_sites, sigma_sites, environment):
@@ -538,7 +609,7 @@
             pltpu.VMEM((pairs, rows, cols), BF16),
             pltpu.VMEM((units + NREM + 1, width, cols), F32),
             pltpu.VMEM(piece, BF16), pltpu.VMEM(piece, BF16), pltpu.VMEM(piece, BF16),
-            pltpu.VMEM(pair, BF16), pltpu.VMEM(pair, BF16), pltpu.VMEM(pair, BF16),
+            pltpu.VMEM(pair, BF16), pltpu.VMEM(pair, BF16), pltpu.VMEM(pair, BF16), pltpu.VMEM(pair, BF16),
             sem((4, NCH)), sem((4, NCH)), sem((4, NCH)), sem((4,)), sem((4,)), sem((4,)), sem((4,)),
             sem((2 + NCH,)), sem, sem,
             sem((4,)), sem((4,)), sem((4,)), sem((4,)), sem((4,)), sem((4,)), sem((4,)),

time: 215 us -> 211 us (0.981); the launches traced: 212 us -> 210 us
  no operation moved by 1% of the time
where the time goes in v2:
time: 211 us; the launch traced here: 210 us
  Pallas kernels  209 us (99%)
    pallas_call x1, Pallas kernels, fused(): pl.pallas_call(kernel, out_shape=pltpu.VMEM(environment.shape, F32), in_s...  209 us

profile of v2, /device:TPU:1, one launch (start us, length us, event | category | flops | bytes accessed | tf_op | source)
XLA Modules:
  0.0 210.4 jit_solution(5927410007099264258)
XLA Ops:
  0.0 209.1 %shard_map.37 = f32[1024,512]{1,0:T(8,128)S(1)} custom-call(bf16[1,4,1024,512]{3,2,1,0:T(8,128)(2,1)} %rho_ref.1, bf16[1,4,1024,512]{3,2,1,0:T(8,128)(2,1)} %sig_ref.1, f32[1024,512]{1,0:T(8,128)} %env_ref.1), custom_call_target="tpu_custom_call" | custom-call | tf_op jit(solution)/shard_map/pallas_call | solution.py:598
  209.1 1.3 copy.5

commit v3 on v2

--- a/solution.py
+++ b/solution.py
@@ -38,9 +38,9 @@
 
 def kernel(rho_ref, sig_ref, env_ref, out_ref,
            rho_g, sig, env_f, env_g, half, half_r, acc, psend, rbuf, s1, f1, s2, f2, zbuf,
-           rl_send, rr_send, r_recv, l_send, l_recv, h_send, h_recv, loc, sg_send, sg_recv,
-           el_send, er_send, e_recv, ex_send, ex_recv, ey_send, ey_recv,
-           row_send, row_recv, x_send, x_recv, y_send, y_recv, z_send, z_recv):
+           r_send, r_recv, p_send, l_recv, h_recv, loc, sg_send, sg_recv,
+           e_send, e_recv, ex_send, ex_recv, ey_send, ey_recv,
+           row_send, row_recv, t_send, t_recv, u_recv):
     ph = lax.axis_index("phys")
     r = lax.axis_index("row")
     c = lax.axis_index("col")
@@ -72,13 +72,16 @@
         return pltpu.make_async_remote_copy(src_ref=src, dst_ref=dst, send_sem=ss, recv_sem=rs,
                                             device_id=dev, device_id_type=MESH)
 
-    load_env = pltpu.make_async_copy(env_ref, env_f, loc.at[0])
-    load_env.start()
-    load_rho = [pltpu.make_async_copy(rho_ref.at[0, :, :, pl.ds(k * width, width)], rho_g.at[c, k], loc.at[1 + k]) for k in range(NCH)]
+    env_parts = [pl.ds(pl.multiple_of((ph + j) % 4 * quarter, quarter), quarter) for j in range(4)]
+    load_env = [pltpu.make_async_copy(env_ref.at[at], env_f.at[at], loc.at[1 + NCH + j]) for j, at in enumerate(env_parts)]
+    load_env[0].start()
+    load_rho = [pltpu.make_async_copy(rho_ref.at[0, :, :, pl.ds(k * width, width)], rho_g.at[c, k], loc.at[k]) for k in range(NCH)]
     for cp in load_rho:
         cp.start()
+    for cp in load_env[1:]:
+        cp.start()
     my_rows = pl.ds(pl.multiple_of(r * rows, rows), rows)
-    load_sig = pltpu.make_async_copy(sig_ref.at[0], sig.at[:, my_rows, :], loc.at[1 + NCH])
+    load_sig = pltpu.make_async_copy(sig_ref.at[0], sig.at[:, my_rows, :], loc.at[NCH])
     load_sig.start()
 
     barrier = pltpu.get_barrier_semaphore()
@@ -93,18 +96,22 @@
     def _():
         pl.semaphore_signal(barrier, inc=1, device_id=right, device_id_type=MESH)
 
-    load_env.wait()
-    env_g[c] = env_f[...].astype(BF16)
+    def cast_env(j):
+        load_env[j].wait()
+        env_g[c, env_parts[j]] = env_f[env_parts[j]].astype(BF16)
+
+    cast_env(0)
     pl.semaphore_wait(barrier, 3 + pick((1, 2, 2, 1)))
 
-    q_rows = pl.ds(pl.multiple_of(ph * quarter, quarter), quarter)
+    q_rows = env_parts[0]
     h_rows = pl.ds(pl.multiple_of((ph // 2) * 2 * quarter, 2 * quarter), 2 * quarter)
 
     def env_left(b):
-        return remote(env_g.at[b, q_rows], env_g.at[b, q_rows], el_send.at[b], e_recv.at[b], left)
-
-    def env_right(b):
-        return remote(env_g.at[b, q_rows], env_g.at[b, q_rows], er_send.at[b], e_recv.at[b], right)
+        return remote(env_g.at[b, q_rows], env_g.at[b, q_rows], e_send.at[b], e_recv.at[b], left)
+
+    def env_right(b, slot=None):
+        slot = b if slot is None else slot
+        return remote(env_g.at[b, q_rows], env_g.at[b, q_rows], e_send.at[slot], e_recv.at[b], right)
 
     def env_x(b):
         return remote(env_g.at[b, q_rows], env_g.at[b, q_rows], ex_send.at[b], ex_recv.at[b], xn)
@@ -113,22 +120,23 @@
         return remote(env_g.at[b, h_rows], env_g.at[b, h_rows], ey_send.at[b], ey_recv.at[b], yn)
 
     def send_left(b, k):
-        return remote(rho_g.at[b, k], rho_g.at[b, k], rl_send.at[b, k], r_recv.at[b, k], left)
-
-    def send_right(b, k):
-        return remote(rho_g.at[b, k], rho_g.at[b, k], rr_send.at[b, k], r_recv.at[b, k], right)
+        return remote(rho_g.at[b, k], rho_g.at[b, k], r_send.at[b, k], r_recv.at[b, k], left)
+
+    def send_right(b, k, slot=None):
+        slot = b if slot is None else slot
+        return remote(rho_g.at[b, k], rho_g.at[b, k], r_send.at[slot, k], r_recv.at[b, k], right)
 
     def first_piece(p):
         at = rho_g.at[c, 0, p]
-        remote(at, at, rl_send.at[c, 0], r_recv.at[c, 0], left).start()
-        remote(at, at, rr_send.at[c, 0], r_recv.at[c, 0], right).start()
+        remote(at, at, r_send.at[c, 0], r_recv.at[c, 0], left).start()
+        remote(at, at, r_send.at[4, 0], r_recv.at[c, 0], right).start()
 
     def pass_piece(b, k, dev):
         at = rho_g.at[b, k, SPLIT]
-        return remote(at, at, rl_send.at[b, k], r_recv.at[b, k], dev)
+        return remote(at, at, r_send.at[b, k], r_recv.at[b, k], dev)
 
     def last_piece(b, p):
-        return remote(rho_g.at[b, NCH - 1, p], rho_g.at[b, NCH - 1, p], l_send.at[p], l_recv.at[p], middle)
+        return remote(rho_g.at[b, NCH - 1, p], rho_g.at[b, NCH - 1, p], p_send.at[p], l_recv.at[p], middle)
 
     @pl.when(c > 0)
     def _():
@@ -136,7 +144,7 @@
 
     @pl.when(c < 3)
     def _():
-        env_right(c).start()
+        env_right(c, 4).start()
 
     give_sig = remote(sig_ref.at[0], sig.at[:, my_rows, :], sg_send, sg_recv, mate)
     load_rho[0].wait()
@@ -145,6 +153,8 @@
     def _():
         first_piece(0)
     give_sig.start()
+    for j in range(1, 4):
+        cast_env(j)
 
     def first_sends(i, k):
         for b, kk in FIRST_LEFT.get(i, []):
@@ -152,7 +162,7 @@
                 send_left(b, k).start()
         for b, kk in FIRST_RIGHT.get(i, []):
             if kk == k:
-                send_right(b, k).start()
+                send_right(b, k, 4).start()
 
     for k in range(NCH):
         if k:
@@ -244,16 +254,16 @@
         return remote(psend.at[unit], rbuf.at[unit], row_send.at[unit], row_recv.at[unit], mate)
 
     def one_x(u):
-        return remote(s1.at[u, part_a], f1.at[u, part_a], x_send.at[u, 0], x_recv.at[u, 0], xn)
+        return remote(s1.at[u, part_a], f1.at[u, part_a], t_send.at[u], t_recv.at[u], xn)
 
     def one_y(u):
-        return remote(s1.at[u, part_b], f1.at[u, part_b], y_send.at[u, 0], y_recv.at[u, 0], yn)
+        return remote(s1.at[u, part_b], f1.at[u, part_b], t_send.at[u], t_recv.at[u], yn)
 
     def two_y(u):
-        return remote(s2.at[u, part_a], f2.at[u, part_a], y_send.at[u, 1], y_recv.at[u, 1], yn)
+        return remote(s2.at[u, part_a], f2.at[u, part_a], t_send.at[u], u_recv.at[u], yn)
 
     def two_x(u):
-        return remote(s2.at[u, part_b], f2.at[u, part_b], x_send.at[u, 1], x_recv.at[u, 1], xn)
+        return remote(s2.at[u, part_b], f2.at[u, part_b], t_send.at[u], u_recv.at[u], xn)
 
     def end_chunk(q):
         b, k = FOR_END[q]
@@ -265,7 +275,7 @@
         return pick((there, there, mirrored, mirrored))
 
     def z_copy(q):
-        return remote(s1.at[2 * NCH + q], zbuf.at[end_unit(q)], z_send.at[q], z_recv.at[q], end)
+        return remote(s1.at[2 * NCH + q], zbuf.at[end_unit(q)], row_send.at[2 * NCH + q], row_recv.at[2 * NCH + q], end)
 
     def end_piece(q):
         return pass_piece(*end_chunk(q), end)
@@ -308,16 +318,14 @@
         one_y(u).start()
 
     def turn(u):
-        one_x(u).wait_recv()
+        remote(s1.at[u], f1.at[u], t_send.at[u], t_recv.at[u], xn).wait_recv()
         s2[u, part_a] = (s1[u, part_a].astype(F32) + f1[u, part_a].astype(F32)).astype(BF16)
         two_y(u).start()
-        one_y(u).wait_recv()
         s2[u, part_b] = (s1[u, part_b].astype(F32) + f1[u, part_b].astype(F32)).astype(BF16)
         two_x(u).start()
 
     def finish(u):
-        two_y(u).wait_recv()
-        two_x(u).wait_recv()
+        remote(s2.at[u], f2.at[u], t_send.at[u], u_recv.at[u], xn).wait_recv()
         at = pl.ds(pl.multiple_of(u * width, width), width)
         out_ref[at, :] = s2[u].astype(F32) + f2[u].astype(F32)
 
@@ -346,7 +354,7 @@
             owned(line[n - 6], finish)
 
     def half_copy(p, dev):
-        return remote(half.at[p], half_r.at[p], h_send.at[p], h_recv.at[p], dev)
+        return remote(half.at[p], half_r.at[p], p_send.at[p], h_recv.at[p], dev)
 
     true = c >= 0
 
@@ -440,10 +448,8 @@
     keeper = jnp.logical_or(jnp.logical_and(c == 0, r == 1), jnp.logical_and(c == 3, r == 0))
 
     def exchanged(u):
-        one_x(u).wait_send()
-        one_y(u).wait_send()
-        two_y(u).wait_send()
-        two_x(u).wait_send()
+        both = s1.at[pl.ds(0, 2)]
+        remote(both, both, t_send.at[u], t_recv.at[u], xn).wait_send()
 
     def sent(pos):
         @pl.when(pos[0])
@@ -470,7 +476,7 @@
 
         @pl.when(c < 3)
         def _():
-            env_right(c).wait_send()
+            env_right(c, 4).wait_send()
         for d in range(1, 4):
             @pl.when(c >= d)
             def _(b=c - d):
@@ -490,13 +496,15 @@
         for i in range(4):
             @pl.when(c == i)
             def _():
-                for first, passed, send in ((FIRST_LEFT, PASS_LEFT, send_left), (FIRST_RIGHT, PASS_RIGHT, send_right)):
-                    todo = list(first.get(i, []))
+                for b, k in FIRST_LEFT.get(i, []):
+                    send_left(b, k).wait_send()
+                for b, k in FIRST_RIGHT.get(i, []):
+                    send_right(b, k, 4).wait_send()
+                for passed, send in ((PASS_LEFT, send_left), (PASS_RIGHT, send_right)):
                     for (j, t), v in passed.items():
-                        if j == i:
-                            todo += [(b, k) for b, k in v if b != i]
-                    for b, k in todo:
-                        send(b, k).wait_send()
+                        for b, k in v:
+                            if j == i and b != i:
+                                send(b, k).wait_send()
                 if i in (0, 3):
                     for p in range(SPLIT):
                         half_copy(p, right if i == 0 else left).wait_send()
@@ -610,12 +618,11 @@
             pltpu.VMEM((units + NREM + 1, width, cols), F32),
             pltpu.VMEM(piece, BF16), pltpu.VMEM(piece, BF16), pltpu.VMEM(piece, BF16),
             pltpu.VMEM(pair, BF16), pltpu.VMEM(pair, BF16), pltpu.VMEM(pair, BF16), pltpu.VMEM(pair, BF16),
-            sem((4, NCH)), sem((4, NCH)), sem((4, NCH)), sem((4,)), sem((4,)), sem((4,)), sem((4,)),
-            sem((2 + NCH,)), sem, sem,
-            sem((4,)), sem((4,)), sem((4,)), sem((4,)), sem((4,)), sem((4,)), sem((4,)),
+            sem((5, NCH)), sem((4, NCH)), sem((4,)), sem((4,)), sem((SPLIT,)),
+            sem((5 + NCH,)), sem, sem,
+            sem((5,)), sem((4,)), sem((4,)), sem((4,)), sem((4,)), sem((4,)),
             sem((units + NREM,)), sem((units + NREM,)),
-            sem((units, 2)), sem((units, 2)), sem((units, 2)), sem((units, 2)),
-            sem((NREM,)), sem((NREM,)),
+            sem((units,)), sem((units,)), sem((units,)),
         ],
         compiler_params=pltpu.CompilerParams(
             collective_id=0, has_side_effects=True, vmem_limit_bytes=58 * 1024 * 1024

time: 211 us -> 210 us (level)
  no operation moved by 1% of the time
where the time goes in v3:
time: 210 us
  Pallas kernels  208 us (99%)
    pallas_call x1, Pallas kernels, fused(): pl.pallas_call(kernel, out_shape=pltpu.VMEM(environment.shape, F32), in_s...  208 us

profile of v3, /device:TPU:1, one launch (start us, length us, event | category | flops | bytes accessed | tf_op | source)
XLA Modules:
  0.0 209.6 jit_solution(208969633860165887)
XLA Ops:
  0.0 208.3 %shard_map.37 = f32[1024,512]{1,0:T(8,128)S(1)} custom-call(bf16[1,4,1024,512]{3,2,1,0:T(8,128)(2,1)} %rho_ref.1, bf16[1,4,1024,512]{3,2,1,0:T(8,128)(2,1)} %sig_ref.1, f32[1024,512]{1,0:T(8,128)} %env_ref.1), custom_call_target="tpu_custom_call" | custom-call | tf_op jit(solution)/shard_map/pallas_call | solution.py:606
  208.3 1.3 copy.5

commit v4 on v3

--- a/solution.py
+++ b/solution.py
@@ -31,13 +31,14 @@
 FOR_END = [(2, 0), (2, 1), (2, 2), (3, 0), (3, 1), (3, 2), (3, 3), (2, 3)]
 NREM = len(FOR_END)
 SPLIT = 3
-LAST_ORDER = (3, 0, 1, 2)
+LAST = 7
+PARTS = 4
 F32 = jnp.float32
 BF16 = jnp.bfloat16
 
 
 def kernel(rho_ref, sig_ref, env_ref, out_ref,
-           rho_g, sig, env_f, env_g, half, half_r, acc, psend, rbuf, s1, f1, s2, f2, zbuf,
+           rho_g, sig, env_f, env_g, half, half_r, acc, psend, rbuf, s1, f1, s2, f2, zbuf, pk_far, pk_mid,
            r_send, r_recv, p_send, l_recv, h_recv, loc, sg_send, sg_recv,
            e_send, e_recv, ex_send, ex_recv, ey_send, ey_recv,
            row_send, row_recv, t_send, t_recv, u_recv):
@@ -47,6 +48,8 @@
     width = rho_g.shape[-1]
     rows = rho_g.shape[3]
     quarter = rows // 4
+    group = rows // PARTS
+    lanes = width // PARTS
     ind3 = c // 3
     ind2 = c // 2 - ind3
     ind0 = (3 - c) // 3
@@ -135,8 +138,14 @@
         at = rho_g.at[b, k, SPLIT]
         return remote(at, at, r_send.at[b, k], r_recv.at[b, k], dev)
 
-    def last_piece(b, p):
-        return remote(rho_g.at[b, NCH - 1, p], rho_g.at[b, NCH - 1, p], p_send.at[p], l_recv.at[p], middle)
+    def last_piece(n):
+        if n == 0:
+            src, dst = pk_far.at[0], pk_far.at[1]
+        elif n < PARTS:
+            src, dst = pk_mid.at[0, n - 1], pk_mid.at[1, n - 1]
+        else:
+            src, dst = pk_mid.at[0, PARTS - 1, n - PARTS], pk_mid.at[1, PARTS - 1, n - PARTS]
+        return remote(src, dst, p_send.at[n], l_recv.at[n], middle)
 
     @pl.when(c > 0)
     def _():
@@ -247,23 +256,35 @@
             acc[unit] += lax.dot_general(rho_g[b, k, p], other[p], (((0,), (0,)), ((), ())),
                                          preferred_element_type=F32)
 
-    part_a = pl.ds(0, width // 2)
-    part_b = pl.ds(width // 2, width // 2)
-
     def row_copy(unit):
         return remote(psend.at[unit], rbuf.at[unit], row_send.at[unit], row_recv.at[unit], mate)
 
-    def one_x(u):
-        return remote(s1.at[u, part_a], f1.at[u, part_a], t_send.at[u], t_recv.at[u], xn)
-
-    def one_y(u):
-        return remote(s1.at[u, part_b], f1.at[u, part_b], t_send.at[u], t_recv.at[u], yn)
-
-    def two_y(u):
-        return remote(s2.at[u, part_a], f2.at[u, part_a], t_send.at[u], u_recv.at[u], yn)
-
-    def two_x(u):
-        return remote(s2.at[u, part_b], f2.at[u, part_b], t_send.at[u], u_recv.at[u], xn)
+    whole = (0, width)
+    main = (0, width - lanes)
+    rest = (width - lanes, lanes)
+
+    def halves(part):
+        lo, n = part
+        return pl.ds(lo, n // 2), pl.ds(lo + n // 2, n // 2)
+
+    def lane_of(u, part):
+        return 2 * NCH if part is rest else u
+
+    def one_x(u, part):
+        at, i = halves(part)[0], lane_of(u, part)
+        return remote(s1.at[u, at], f1.at[u, at], t_send.at[i], t_recv.at[i], xn)
+
+    def one_y(u, part):
+        at, i = halves(part)[1], lane_of(u, part)
+        return remote(s1.at[u, at], f1.at[u, at], t_send.at[i], t_recv.at[i], yn)
+
+    def two_y(u, part):
+        at, i = halves(part)[0], lane_of(u, part)
+        return remote(s2.at[u, at], f2.at[u, at], t_send.at[i], u_recv.at[i], yn)
+
+    def two_x(u, part):
+        at, i = halves(part)[1], lane_of(u, part)
+        return remote(s2.at[u, at], f2.at[u, at], t_send.at[i], u_recv.at[i], xn)
 
     def end_chunk(q):
         b, k = FOR_END[q]
@@ -313,21 +334,22 @@
         def _():
             f(unit_at(pos))
 
-    def begin(u):
-        one_x(u).start()
-        one_y(u).start()
-
-    def turn(u):
-        remote(s1.at[u], f1.at[u], t_send.at[u], t_recv.at[u], xn).wait_recv()
-        s2[u, part_a] = (s1[u, part_a].astype(F32) + f1[u, part_a].astype(F32)).astype(BF16)
-        two_y(u).start()
-        s2[u, part_b] = (s1[u, part_b].astype(F32) + f1[u, part_b].astype(F32)).astype(BF16)
-        two_x(u).start()
-
-    def finish(u):
-        remote(s2.at[u], f2.at[u], t_send.at[u], u_recv.at[u], xn).wait_recv()
-        at = pl.ds(pl.multiple_of(u * width, width), width)
-        out_ref[at, :] = s2[u].astype(F32) + f2[u].astype(F32)
+    def begin(u, part=whole):
+        one_x(u, part).start()
+        one_y(u, part).start()
+
+    def turn(u, part=whole):
+        at, i = pl.ds(*part), lane_of(u, part)
+        remote(s1.at[u, at], f1.at[u, at], t_send.at[i], t_recv.at[i], xn).wait_recv()
+        for at, copy in zip(halves(part), (two_y, two_x)):
+            s2[u, at] = (s1[u, at].astype(F32) + f1[u, at].astype(F32)).astype(BF16)
+            copy(u, part).start()
+
+    def finish(u, part=whole):
+        at, i = pl.ds(*part), lane_of(u, part)
+        remote(s2.at[u, at], f2.at[u, at], t_send.at[i], u_recv.at[i], xn).wait_recv()
+        to = pl.ds(pl.multiple_of(u * width, width) + part[0], part[1])
+        out_ref[to, :] = s2[u, at].astype(F32) + f2[u, at].astype(F32)
 
     def stage1(pos):
         def f(unit):
@@ -374,8 +396,8 @@
                             pass_piece(item[1], item[2], end).start()
                         for b, k in passed.get((i, t), []):
                             if b == i:
-                                for p in LAST_ORDER:
-                                    last_piece(c, p).start()
+                                for n in range(LAST):
+                                    last_piece(n).start()
                             else:
                                 send(b, k).start()
 
@@ -398,6 +420,36 @@
     arrive(1)
     for k in range(NCH):
         advance((true, c, k, None))
+
+    lane = lax.broadcasted_iota(jnp.int32, (group, width), 1) // lanes
+
+    def repacked(p, j):
+        total = None
+        for g in range(PARTS):
+            x = rho_g[c, NCH - 1, p, pl.ds(g * group, group), :].astype(F32)
+            shift = (g - j) * lanes % width
+            if shift:
+                x = pltpu.roll(x, shift, 1)
+            total = x if g == 0 else jnp.where(lane == g, x, total)
+        return total.astype(BF16)
+
+    @pl.when(mid)
+    def _():
+        @pl.loop(0, SPLIT)
+        def _(p):
+            for j in range(PARTS):
+                pk_mid[0, j, p] = repacked(p, j)
+        for j in range(PARTS):
+            pk_far[0, j] = repacked(SPLIT, j)
+
+    def packed_product(lhs, other, p, slot, j):
+        total = 0
+        for g in range(PARTS):
+            part = lax.dot_general(lhs[...], other[p, pl.ds(g * group, group), :], (((0,), (0,)), ((), ())),
+                                   preferred_element_type=F32)
+            total = total + part[g * lanes:(g + 1) * lanes]
+        at = pl.ds(pl.multiple_of(j * lanes, lanes), lanes)
+        acc[slot, at] += total
 
     @pl.when(c == 0)
     def _():
@@ -447,9 +499,9 @@
     at_end = jnp.logical_or(c == 0, c == 3)
     keeper = jnp.logical_or(jnp.logical_and(c == 0, r == 1), jnp.logical_and(c == 3, r == 0))
 
-    def exchanged(u):
-        both = s1.at[pl.ds(0, 2)]
-        remote(both, both, t_send.at[u], t_recv.at[u], xn).wait_send()
+    def exchanged(u, part=whole):
+        both, i = s1.at[pl.ds(0, 2), pl.ds(*part)], lane_of(u, part)
+        remote(both, both, t_send.at[i], t_recv.at[i], xn).wait_send()
 
     def sent(pos):
         @pl.when(pos[0])
@@ -516,50 +568,132 @@
     def _():
         settle()
 
-    def last_products(p):
-        last_piece(3 - c, p).wait_recv()
-        first, final = p == LAST_ORDER[0], p == LAST_ORDER[-1]
-        if p == SPLIT:
-            end_piece(NREM - 1).start()
+    def far_piece():
+        return remote(pk_far.at[1], pk_far.at[1], r_send.at[3 - c, NCH - 1], r_recv.at[end_chunk(NREM - 1)[0], NCH - 1], end)
+
+    def row_index(pos, part):
+        if part is main:
+            return unit_at(pos)
+        return 2 * NCH + NREM + (0 if pos[3] is not None else 1)
+
+    def row_part(pos, part):
+        u, at, i = unit_at(pos), pl.ds(*part), row_index(pos, part)
+        return remote(psend.at[u, at], rbuf.at[u, at], row_send.at[i], row_recv.at[i], mate)
+
+    def z_part(part):
+        at, i = pl.ds(*part), 2 * NCH + NREM - 1 if part is main else 2 * NCH + NREM
+        q = NREM - 1
+        return remote(s1.at[2 * NCH + q, at], zbuf.at[end_unit(q), at], row_send.at[i], row_recv.at[i], end)
+
+    def to_mate_part(pos, part):
+        @pl.when(pos[1] // 2 != r)
+        def _():
+            at = pl.ds(*part)
+            psend[unit_at(pos), at] = acc[slot_at(pos), at].astype(BF16)
+            row_part(pos, part).start()
+
+    def row_sum(pos, part):
+        at = pl.ds(*part)
+
+        def f(unit):
+            row_part(pos, part).wait_recv()
+            s1[unit, at] = (acc[unit, at] + rbuf[unit, at].astype(F32)).astype(BF16)
+            if pos[3] is None:
+                begin(unit, part)
+            else:
+                z_part(part).start()
+        owned(pos, f)
+
+    def last_products(n):
+        last_piece(n).wait_recv()
+        if n == 0:
+            far_piece().start()
+
+            @pl.loop(0, PARTS)
+            def _(j):
+                packed_product(pk_far.at[1, j], half, SPLIT, slot_at(own_last), j)
+        elif n < PARTS:
+            @pl.loop(0, SPLIT)
+            def _(p):
+                packed_product(pk_mid.at[1, n - 1, p], half_r, p, slot_at(end_last), n - 1)
+                packed_product(pk_mid.at[1, n - 1, p], half, p, slot_at(own_last), n - 1)
         else:
-            product(3 - c, NCH - 1, half_r, slot_at(end_last), p, p + 1)
-        if final:
-            to_mate(end_last)
-        product(3 - c, NCH - 1, half, slot_at(own_last), p, p + 1, zero=first)
-        if final:
-            to_mate(own_last)
+            p = n - PARTS
+            packed_product(pk_mid.at[1, PARTS - 1, p], half_r, p, slot_at(end_last), PARTS - 1)
+            if n == LAST - 1:
+                to_mate_part(end_last, rest)
+            packed_product(pk_mid.at[1, PARTS - 1, p], half, p, slot_at(own_last), PARTS - 1)
+            if n == LAST - 1:
+                to_mate_part(own_last, rest)
 
     @pl.when(mid)
     def _():
         for q in range(6):
             end_piece(q).wait_send()
             sent(for_end(q))
-        for p in LAST_ORDER:
-            last_products(p)
-        stage1(end_last)
-        stage1(own_last)
-        owned(own_last, turn)
-        owned(own_last, finish)
+        for pos in (end_last, own_last):
+            acc[slot_at(pos)] = jnp.zeros_like(acc.at[0])
+        for n in range(PARTS):
+            last_products(n)
+        to_mate_part(end_last, main)
+        to_mate_part(own_last, main)
+        last_products(PARTS)
+        row_sum(end_last, main)
+        row_sum(own_last, main)
+        for n in range(PARTS + 1, LAST):
+            last_products(n)
+        row_sum(end_last, rest)
+        row_sum(own_last, rest)
+        for part in (main, rest):
+            owned(own_last, lambda u: turn(u, part))
+        for part in (main, rest):
+            owned(own_last, lambda u: finish(u, part))
         end_piece(6).wait_send()
-        end_piece(7).wait_send()
+        far_piece().wait_send()
         sent(for_end(6))
-        sent(end_last)
-        sent(own_last)
-        for p in LAST_ORDER:
-            last_piece(c, p).wait_send()
+        for pos in (end_last, own_last):
+            @pl.when(pos[1] // 2 != r)
+            def _():
+                for part in (main, rest):
+                    row_part(pos, part).wait_send()
+
+            @pl.when(pos[1] // 2 == r)
+            def _():
+                for part in (main, rest):
+                    if pos[3] is None:
+                        exchanged(unit_at(pos), part)
+                    else:
+                        z_part(part).wait_send()
+        for n in range(LAST):
+            last_piece(n).wait_send()
+
+    def end_position(q):
+        return (at_end,) + end_chunk(q) + (None,)
 
     def end_part(q):
-        pos = (at_end,) + end_chunk(q) + (None,)
-        end_piece(q).wait_recv()
-        product(pos[1], pos[2], half, slot_at(pos), SPLIT, SPLIT + 1, zero=True)
+        pos = end_position(q)
+        if q < NREM - 1:
+            end_piece(q).wait_recv()
+            product(pos[1], pos[2], half, slot_at(pos), SPLIT, SPLIT + 1, zero=True)
+        else:
+            far_piece().wait_recv()
+            acc[slot_at(pos)] = jnp.zeros_like(acc.at[0])
+
+            @pl.loop(0, PARTS)
+            def _(j):
+                packed_product(pk_far.at[1, j], half, SPLIT, slot_at(pos), j)
         to_mate(pos)
 
-    def gather(q):
-        u = end_unit(q)
-        row_copy(u).wait_recv()
-        z_copy(q).wait_recv()
-        s1[u] = (acc[u] + rbuf[u].astype(F32) + zbuf[u].astype(F32)).astype(BF16)
-        begin(u)
+    def gather(q, part=whole):
+        u, at = end_unit(q), pl.ds(*part)
+        if part is not rest:
+            row_copy(u).wait_recv()
+        if part is whole:
+            z_copy(q).wait_recv()
+        else:
+            z_part(part).wait_recv()
+        s1[u, at] = (acc[u, at] + rbuf[u, at].astype(F32) + zbuf[u, at].astype(F32)).astype(BF16)
+        begin(u, part)
 
     @pl.when(at_end)
     def _():
@@ -578,17 +712,27 @@
                     finish(end_unit(n - 4))
             for q in range(NREM - 2):
                 exchanged(end_unit(q))
-        for q in (NREM - 2, NREM - 1):
-            end_part(q)
+        before, last = NREM - 2, NREM - 1
+        end_part(before)
 
         @pl.when(keeper)
         def _():
-            for q in (NREM - 2, NREM - 1):
-                gather(q)
-                turn(end_unit(q))
-                finish(end_unit(q))
-            for q in (NREM - 2, NREM - 1):
-                exchanged(end_unit(q))
+            gather(before)
+        end_part(last)
+
+        @pl.when(keeper)
+        def _():
+            turn(end_unit(before))
+            gather(last, main)
+            gather(last, rest)
+            for part in (main, rest):
+                turn(end_unit(last), part)
+            finish(end_unit(before))
+            for part in (main, rest):
+                finish(end_unit(last), part)
+            exchanged(end_unit(before))
+            for part in (main, rest):
+                exchanged(end_unit(last), part)
 
         @pl.when(jnp.logical_not(keeper))
         def _():
@@ -618,11 +762,13 @@
             pltpu.VMEM((units + NREM + 1, width, cols), F32),
             pltpu.VMEM(piece, BF16), pltpu.VMEM(piece, BF16), pltpu.VMEM(piece, BF16),
             pltpu.VMEM(pair, BF16), pltpu.VMEM(pair, BF16), pltpu.VMEM(pair, BF16), pltpu.VMEM(pair, BF16),
-            sem((5, NCH)), sem((4, NCH)), sem((4,)), sem((4,)), sem((SPLIT,)),
+            pltpu.VMEM((2, PARTS, rows // PARTS, width), BF16),
+            pltpu.VMEM((2, PARTS, SPLIT, rows // PARTS, width), BF16),
+            sem((5, NCH)), sem((4, NCH)), sem((LAST,)), sem((LAST,)), sem((SPLIT,)),
             sem((5 + NCH,)), sem, sem,
             sem((5,)), sem((4,)), sem((4,)), sem((4,)), sem((4,)), sem((4,)),
-            sem((units + NREM,)), sem((units + NREM,)),
-            sem((units,)), sem((units,)), sem((units,)),
+            sem((units + NREM + 2,)), sem((units + NREM + 2,)),
+            sem((units + 1,)), sem((units + 1,)), sem((units + 1,)),
         ],
         compiler_params=pltpu.CompilerParams(
             collective_id=0, has_side_effects=True, vmem_limit_bytes=58 * 1024 * 1024

time: 210 us -> 207 us (0.986)
    pallas_call x1, Pallas kernels: 208 us -> 206 us  [fused(): pl.pallas_call(kernel, out_shape=pltpu.VMEM(environment.shape, F32), in_s...]
where the time goes in v4:
time: 207 us
  Pallas kernels  206 us (100%)
    pallas_call x1, Pallas kernels, fused(): pl.pallas_call(kernel, out_shape=pltpu.VMEM(environment.shape, F32), in_s...  206 us

profile of v4, /device:TPU:1, one launch (start us, length us, event | category | flops | bytes accessed | tf_op | source)
XLA Modules:
  0.0 207.2 jit_solution(4738344993806508590)
XLA Ops:
  0.0 205.8 %shard_map.37 = f32[1024,512]{1,0:T(8,128)S(1)} custom-call(bf16[1,4,1024,512]{3,2,1,0:T(8,128)(2,1)} %rho_ref.1, bf16[1,4,1024,512]{3,2,1,0:T(8,128)(2,1)} %sig_ref.1, f32[1024,512]{1,0:T(8,128)} %env_ref.1), custom_call_target="tpu_custom_call" | custom-call | tf_op jit(solution)/shard_map/pallas_call | solution.py:750
  205.9 1.3 copy.5
